TPU v7x, 32 devices: a whole 2x2x4 slice. The times are simulated.
32 devices in a mesh: row: 4 (over y, x), col: 8 (over z, core).
Axes of the slice: x: 2, y: 2, z: 4, core: 2. Of those that a mesh axis runs over, the one named last changes fastest.
Arguments:
- inverse: float32 [24576, 24576], P('row', 'col'), may hold values from -0.0546875 to 0.0546875
- parent_panel: float32 [24576, 256], P(('row', 'col')), may hold values from -1.8 to 1.8
- child_panel: float32 [24576, 256], P(('row', 'col')), may hold values from -1.8 to 1.8
- child_top: float32 [256, 256], replicated, may hold values from -0.375 to 0.375
- diag_parent: float32 [256, 256], replicated, may hold values from -12 to 12
- diag_child: float32 [256, 256], replicated, may hold values from -12 to 12
- parent_blocks: int32 [192], replicated, may hold values from 0 to 1
- child_blocks: int32 [192], replicated, may hold values from 0 to 1, as said below
Outputs:
- parent_column: float32 [24576, 256], P(('row', 'col'))
- parent_diagonal: float32 [256, 256], replicated
- child_column: float32 [24576, 256], P(('row', 'col'))
- child_upper: float32 [256, 256], replicated
- child_diagonal: float32 [256, 256], replicated
Inputs may be any that keep to these rules, and one draw needn't show every extreme that they name: `child_blocks`: each entry is 0 or 1, and is 1 only where parent_blocks is 1.
All inputs are finite; a program needn't handle non-finite values.
Results may differ from a plain program's by a relative error of at most 0.000086.
Values sent between devices are 32-bit elements; how exact they have to be, the bound alone decides.
A program may use at most 192 MiB of HBM per device.

v0:
```python
import jax
import jax.numpy as jnp
from jax import lax
from jax.sharding import PartitionSpec as P

BLK = 128
HIGHEST = lax.Precision.HIGHEST


def spread(value, axis, source):
    kept = jnp.where(lax.axis_index(axis) == source, value, 0).astype(value.dtype)
    return lax.psum(kept, axis)


def matmul(left, right):
    return jnp.dot(left, right, precision=HIGHEST, preferred_element_type=jnp.float32)


def local_mask(blocks, rows_here):
    flags = jnp.repeat(blocks, BLK, total_repeat_length=blocks.shape[0] * BLK)
    device = lax.axis_index("row") * lax.axis_size("col") + lax.axis_index("col")
    local_flags = lax.dynamic_slice_in_dim(flags, device * rows_here, rows_here, 0)
    return local_flags.astype(jnp.float32)[:, None]


def column_slice(block_rows, tile_cols):
    col_ratio = lax.axis_size("col") // lax.axis_size("row")
    index_col = lax.axis_index("col")
    wanted = lax.dynamic_slice_in_dim(block_rows, index_col % col_ratio * tile_cols, tile_cols, 0)
    return (wanted, index_col // col_ratio)


def apply_inverse(inverse, panel):
    rows_here = panel.shape[0]
    block_rows = lax.all_gather(panel, "col", axis=0, tiled=True)
    wanted, owner_row = column_slice(block_rows, inverse.shape[1])
    column_rows = spread(wanted, "row", owner_row)
    return lax.psum_scatter(
        matmul(lax.slice_in_dim(inverse, 0, rows_here * lax.axis_size("col"), axis=0), column_rows),
        "col",
        scatter_dimension=0,
        tiled=True,
    )


def per_device(
    inverse,
    parent_panel,
    child_panel,
    child_top,
    diag_parent,
    diag_child,
    parent_blocks,
    child_blocks,
):
    rows_here = parent_panel.shape[0]
    parent_mask = local_mask(parent_blocks, rows_here)
    child_mask = local_mask(child_blocks, rows_here)
    parent_masked = parent_panel * parent_mask
    child_masked = child_panel * child_mask
    parent_image = apply_inverse(inverse, parent_masked)
    child_image = apply_inverse(inverse, child_masked)
    parent_column = -(parent_mask * parent_image)
    parent_local = matmul(parent_masked.T, parent_column)
    cross_local = matmul(parent_column.T, child_masked)
    carried = matmul(parent_column, child_top)
    child_column = -(child_mask * (carried + child_image))
    image_local = matmul(child_masked.T, child_image)
    parent_sum, cross_sum, image_sum = lax.psum(
        (parent_local, cross_local, image_local), ("row", "col")
    )
    parent_diagonal = diag_parent - parent_sum
    child_upper = -(matmul(parent_diagonal, child_top) + cross_sum)
    child_diagonal = (
        diag_child - matmul(child_top.T, child_upper) + matmul(cross_sum.T, child_top) + image_sum
    )
    return (parent_column, parent_diagonal, child_column, child_upper, child_diagonal)


def solution(mesh):
    placed = (
        P("row", "col"),
        P(("row", "col"), None),
        P(("row", "col"), None),
        P(),
        P(),
        P(),
        P(),
        P(),
    )
    return jax.shard_map(
        per_device,
        mesh=mesh,
        in_specs=placed,
        out_specs=(P(("row", "col"), None), P(), P(("row", "col"), None), P(), P()),
        check_vma=False,
    )
```

profile of v0, /device:TPU:0, one launch (start us, length us, event | category | flops | bytes accessed | tf_op | source)
XLA Modules:
  0.0 949.8 jit_solution(11591505820948566814)
XLA Ops:
  7.2 0.0 copy-start
  7.2 0.0 copy-start.1
  7.2 0.0 all-gather.5.cloned.1.call-start
  7.3 0.8 add_bitcast_fusion.1
  8.0 1.9 scatter_custom_fusion
  9.9 0.1 copy.22
  10.0 0.2 reduce-window.20
  10.2 0.3 reduce-window.21
  10.5 0.1 slice.44
  10.6 0.1 slice_reduce_fusion
  10.7 0.1 add_bitcast_fusion
  10.8 0.1 pad_slice_fusion
  10.9 0.1 copy.23
  11.1 0.0 copy-start.2
  11.1 151.8 %gather_fusion = s32[24576]{0:T(1024)S(1)} fusion(s32[192]{0:T(256)S(1)} %copy-done.1, s32[24576]{0:T(1024)S(1)} %fusion.5), kind=kCustom, calls=%fused_computation.clone | custom fusion | bytes 294912 | tf_op jit(solution)/shard_map/jit(_take)/gather | solution.py:20
  162.9 0.0 copy-start.9
  162.9 151.8 %gather_fusion.1 = s32[24576]{0:T(1024)S(1)} fusion(s32[192]{0:T(256)S(1)} %copy-done.2, s32[24576]{0:T(1024)S(1)} %fusion.5), kind=kCustom, calls=%fused_computation.1.clone | custom fusion | bytes 294912 | tf_op jit(solution)/shard_map/jit(_take)/gather | solution.py:20
  314.8 0.0 copy-start.10
  314.8 0.3 copy.25
  315.1 0.1 fusion.8
  315.1 0.9 broadcast_multiply_fusion
  316.1 0.0 all-gather.5.cloned.1.call-update
  316.1 0.0 all-gather.3.cloned.1.call-start
  316.2 0.3 copy.24
  316.4 0.9 broadcast_multiply_fusion.1
  317.4 0.0 all-gather.3.cloned.1.call-update
  317.4 0.0 all-reduce.9.cloned.1.call-start
  317.5 66.2 %all-gather.5.cloned.1.call-done = f32[6144,256]{0,1:T(8,128)} async-done(((f32[768,256]{0,1:T(8,128)}), f32[6144,256]{0,1:T(8,128)}) %all-gather.5.cloned.1.call-update) | async-done | bytes 6291472 | tf_op jit(solution)/shard_map/all_gather | solution.py:35
  383.7 3.8 dynamic-slice_select_fusion
  387.5 61.7 %all-gather.3.cloned.1.call-done = f32[6144,256]{0,1:T(8,128)} async-done(((f32[768,256]{0,1:T(8,128)}), f32[6144,256]{0,1:T(8,128)}) %all-gather.3.cloned.1.call-update) | async-done | bytes 6291472 | tf_op jit(solution)/shard_map/all_gather | solution.py:35
  449.2 3.9 dynamic-slice_select_fusion.1
  453.1 0.0 all-reduce.9.cloned.1.call-update
  453.1 0.0 reduce-scatter.3.cloned.1.call-start
  453.2 136.9 %all-reduce.9.cloned.1.call-done = (f32[3072,256]{0,1:T(8,128)}, f32[3072,256]{0,1:T(8,128)}) async-done(((f32[3072,256]{0,1:T(8,128)}, f32[3072,256]{0,1:T(8,128)}), (f32[3072,256]{0,1:T(8,128)}, f32[3072,256]{0,1:T(8,128)})) %all-reduce.9.cloned.1.call-update) | async-done | bytes 6291472 | tf_op jit(solution)/shard_map/psum | solution.py:12
  590.1 70.0 %convolution_bitcast_fusion.1 = f32[6144,256]{0,1:T(8,128)} fusion(f32[3072,256]{0,1:T(8,128)} %get-tuple-element.39, f32[6144,3072]{1,0:T(8,128)} %param.14), kind=kOutput, calls=%fused_computation.4 | convolution fusion | flops 57982058496 | bytes 84934656 | tf_op jit(solution)/shard_map/dot_general | solution.py:16
  660.1 0.0 reduce-scatter.3.cloned.1.call-update
  660.1 0.2 reduce-scatter.5.cloned.1.call-start
  660.4 1.6 copy-done.5
  662.0 70.3 %convolution_bitcast_fusion = f32[6144,256]{0,1:T(8,128)} fusion(f32[3072,256]{0,1:T(8,128)S(1)} %copy-done.5, f32[6144,3072]{1,0:T(8,128)} %param.14), kind=kOutput, calls=%fused_computation.3 | convolution fusion | flops 57982058496 | bytes 84934656 | tf_op jit(solution)/shard_map/dot_general | solution.py:16
  732.3 0.0 reduce-scatter.5.cloned.1.call-update
  732.3 0.0 copy-start.4
  732.3 0.3 all-reduce.7.cloned.1.call-start
  732.6 0.0 reduce-scatter.3.cloned.1.call-done
  732.6 1.3 multiply_negate_fusion
  733.9 0.0 copy-done.3
  733.9 0.0 copy-start.12
  733.9 1.5 fusion.11
  735.5 1.5 fusion.10
  737.0 64.8 %reduce-scatter.5.cloned.1.call-done = f32[768,256]{0,1:T(8,128)} async-done(((f32[6144,256]{0,1:T(8,128)}), f32[768,256]{0,1:T(8,128)}) %reduce-scatter.5.cloned.1.call-update) | async-done | bytes 786448 | tf_op jit(solution)/shard_map/reduce_scatter | solution.py:38
  801.8 2.7 fusion.12
  804.6 0.0 all-reduce.7.cloned.1.call-update
  804.6 0.0 copy-start.11
  804.6 0.1 copy.27
  804.8 1.1 copy.30
  805.9 0.9 fusion.1
  806.8 1.1 copy.31
  808.0 129.5 %all-reduce.7.cloned.1.call-done = (f32[256,256]{1,0:T(8,128)}, f32[256,256]{1,0:T(8,128)}, f32[256,256]{0,1:T(8,128)}) async-done(((f32[256,256]{1,0:T(8,128)}, f32[256,256]{1,0:T(8,128)}, f32[256,256]{0,1:T(8,128)}), (f32[256,256]{1,0:T(8,128)}, f32[256,256]{1,0:T(8,128)}, f32[256,256]{0,1:T(8,128)})) %all-reduce.7.cloned.1.call-update) | async-done | bytes 786448 | tf_op jit(solution)/shard_map/psum | solution.py:69
  937.5 1.0 sub.20
  938.4 0.0 copy-start.7
  938.4 1.4 fusion.4
  939.9 0.0 copy-start.8
  939.9 0.6 fusion.3
  940.5 1.6 fusion.2
  942.1 0.8 copy.32
  (23 shorter events, 0.2 us)
Async XLA Ops:
  7.2 798.7 %copy-start = (f32[256,256]{1,0:T(8,128)S(1)}, f32[256,256]{1,0:T(8,128)}, u32[]{:S(2)}) copy-start(f32[256,256]{1,0:T(8,128)} %param.17) | copy-start | bytes 786436
  7.2 3.9 copy-start.1
  7.2 376.5 %all-gather.5.cloned.1.call-start = ((), (), s32[]{:S(2)}) async-start(), calls=%async_computation.4 | async-start | bytes 7077888 | tf_op jit(solution)/shard_map/all_gather | solution.py:35
  11.1 151.8 %copy-start.2 = (s32[192]{0:T(256)S(1)}, s32[192]{0:T(256)}, u32[]{:S(2)}) copy-start(s32[192]{0:T(256)} %param.21) | copy-start | bytes 2308
  162.9 151.8 %copy-start.9 = (f32[768,256]{1,0:T(8,128)S(1)}, f32[768,256]{1,0:T(8,128)}, u32[]{:S(2)}) copy-start(f32[768,256]{1,0:T(8,128)} %param.16) | copy-start | bytes 2359300
  314.8 1.4 copy-start.10
  316.1 133.1 %all-gather.3.cloned.1.call-start = ((), (), s32[]{:S(2)}) async-start(), calls=%async_computation.2 | async-start | bytes 7077888 | tf_op jit(solution)/shard_map/all_gather | solution.py:35
  317.4 272.7 %all-reduce.9.cloned.1.call-start = ((), (), s32[]{:S(2)}) async-start(), calls=%async_computation.7 | async-start | bytes 12582912 | tf_op jit(solution)/shard_map/psum | solution.py:12
  453.1 279.4 %reduce-scatter.3.cloned.1.call-start = ((), (), s32[]{:S(2)}) async-start(), calls=%async_computation.3 | async-start | bytes 7077888 | tf_op jit(solution)/shard_map/reduce_scatter | solution.py:38
  660.1 1.9 copy-start.5
  660.1 141.7 %reduce-scatter.5.cloned.1.call-start = ((), (), s32[]{:S(2)}) async-start(), calls=%async_computation.5 | async-start | bytes 7077888 | tf_op jit(solution)/shard_map/reduce_scatter | solution.py:38
  732.3 1.7 copy-start.3
  732.3 3.2 copy-start.4
  732.3 205.2 %all-reduce.7.cloned.1.call-start = ((), (), s32[]{:S(2)}) async-start(), calls=%async_computation.6 | async-start | bytes 1572864 | tf_op jit(solution)/shard_map/psum | solution.py:69
  733.9 70.7 %copy-start.12 = (f32[256,256]{1,0:T(8,128)S(1)}, f32[256,256]{1,0:T(8,128)}, u32[]{:S(2)}) copy-start(f32[256,256]{1,0:T(8,128)} %param.19) | copy-start | bytes 786436
  801.8 4.1 copy-start.6
  804.6 132.8 %copy-start.11 = (f32[256,256]{1,0:T(8,128)S(1)}, f32[256,256]{1,0:T(8,128)}, u32[]{:S(2)}) copy-start(f32[256,256]{1,0:T(8,128)} %param.18) | copy-start | bytes 786436
  938.4 4.5 copy-start.7
  939.9 3.1 copy-start.8
Sparse Core Ops, SparseCore 0:
  316.2 67.4 all-gather.4
  385.9 63.3 all-gather.2
  453.3 136.7 all-reduce.8
  660.2 69.7 reduce-scatter.2
  732.4 69.4 reduce-scatter.4
  807.8 129.6 all-reduce.6
where the time goes:
time: 950 us
  waiting for transfers between devices  459 us (48%)
  local copies, waits for them, and re-layouts  310 us (33%)
  matrix products  151 us (16%)
  other arithmetic  15.3 us (2%)
  between operations  14.4 us (2%)
    gather x2, local copies, waits for them, and re-layouts, local_mask(): flags = jnp.repeat(blocks, BLK, total_repeat_length=blocks.shape[0] * BLK)  304 us
    dot_general x9, matrix products, matmul(): jnp.dot(left, right, precision=HIGHEST, preferred_element_type=jnp.float32)  151 us
    psum x1, waiting for transfers between devices, spread(): return lax.psum(kept, axis)  137 us
    psum x1, waiting for transfers between devices, per_device(): lax.psum((parent_local, cross_local, image_local), ('row', 'col'))  129 us
    all_gather x2, waiting for transfers between devices, apply_inverse(): block_rows = lax.all_gather(panel, 'col', axis=0, tiled=True)  128 us
    reduce_scatter x2, waiting for transfers between devices, apply_inverse(): lax.psum_scatter(matmul(lax.slice_in_dim(inverse, 0, rows_here * lax.axis...  64.9 us
  transfers between devices with their start and end apart: 6, of which 5 were waited for; matrix products, arithmetic and copies ran while one was open for 9% of the time, Pallas kernels for 0%

commit v1 on v0

--- a/solution.py
+++ b/solution.py
@@ -9,7 +9,7 @@
 
 def spread(value, axis, source):
     kept = jnp.where(lax.axis_index(axis) == source, value, 0).astype(value.dtype)
-    return lax.psum(kept, axis)
+    return jnp.sum(lax.all_gather(kept, axis), axis=0)
 
 
 def matmul(left, right):

time: 950 us -> 1010 us (1.063)
  local copies, waits for them, and re-layouts: 310 us -> 339 us
  other arithmetic: 15.3 us -> 35.2 us
    all_gather x0 -> x2, waiting for transfers between devices: none -> 147 us  [spread(): return jnp.sum(lax.all_gather(kept, axis), axis=0)]
    psum x1 -> x0, waiting for transfers between devices: 137 us -> none  [spread(): return lax.psum(kept, axis)]
    all_gather x0 -> x2, local copies, waits for them, and re-layouts: none -> 31.4 us  [spread(): return jnp.sum(lax.all_gather(kept, axis), axis=0)]
    reduce_sum x0 -> x2, other arithmetic: none -> 19.8 us  [spread(): return jnp.sum(lax.all_gather(kept, axis), axis=0)]
  transfers between devices with their start and end apart: 6 -> 7, of which waited for: 5 -> 6; matrix products, arithmetic and copies ran while one was open for 9% -> 21% of each run, Pallas kernels for 0% -> 0%
where the time goes in v1:
time: 1010 us
  waiting for transfers between devices  469 us (46%)
  local copies, waits for them, and re-layouts  339 us (34%)
  matrix products  152 us (15%)
  other arithmetic  35.2 us (3%)
  between operations  14.4 us (1%)
    gather x2, local copies, waits for them, and re-layouts, local_mask(): flags = jnp.repeat(blocks, BLK, total_repeat_length=blocks.shape[0] * BLK)  304 us
    dot_general x9, matrix products, matmul(): jnp.dot(left, right, precision=HIGHEST, preferred_element_type=jnp.float32)  152 us
    all_gather x2, waiting for transfers between devices, spread(): return jnp.sum(lax.all_gather(kept, axis), axis=0)  147 us
    psum x1, waiting for transfers between devices, per_device(): lax.psum((parent_local, cross_local, image_local), ('row', 'col'))  129 us
    all_gather x2, waiting for transfers between devices, apply_inverse(): block_rows = lax.all_gather(panel, 'col', axis=0, tiled=True)  128 us
    reduce_scatter x2, waiting for transfers between devices, apply_inverse(): lax.psum_scatter(matmul(lax.slice_in_dim(inverse, 0, rows_here * lax.axis...  65.2 us
    all_gather x2, local copies, waits for them, and re-layouts, spread(): return jnp.sum(lax.all_gather(kept, axis), axis=0)  31.4 us
  transfers between devices with their start and end apart: 7, of which 6 were waited for; matrix products, arithmetic and copies ran while one was open for 21% of the time, Pallas kernels for 0%

profile of v1, /device:TPU:0, one launch (start us, length us, event | category | flops | bytes accessed | tf_op | source)
XLA Modules:
  0.0 1009.9 jit_solution(2501764447730200692)
XLA Ops:
  7.2 0.0 copy-start
  7.2 0.0 all-gather.7.cloned.1.call-start
  7.3 0.8 add_bitcast_fusion.1
  8.0 1.9 scatter_custom_fusion
  9.9 0.1 copy.33
  10.0 0.2 reduce-window.20
  10.2 0.3 reduce-window.21
  10.5 0.1 slice.44
  10.6 0.1 slice_reduce_fusion
  10.7 0.1 add_bitcast_fusion
  10.8 0.1 pad_slice_fusion
  10.9 0.1 copy.34
  11.1 0.0 copy-start.2
  11.1 151.8 %gather_fusion = s32[24576]{0:T(1024)S(1)} fusion(s32[192]{0:T(256)S(1)} %copy-done.1, s32[24576]{0:T(1024)S(1)} %fusion.5), kind=kCustom, calls=%fused_computation.clone | custom fusion | bytes 294912 | tf_op jit(solution)/shard_map/jit(_take)/gather | solution.py:20
  162.9 0.0 copy-start.8
  163.0 151.8 %gather_fusion.1 = s32[24576]{0:T(1024)S(1)} fusion(s32[192]{0:T(256)S(1)} %copy-done.2, s32[24576]{0:T(1024)S(1)} %fusion.5), kind=kCustom, calls=%fused_computation.1.clone | custom fusion | bytes 294912 | tf_op jit(solution)/shard_map/jit(_take)/gather | solution.py:20
  314.8 0.3 copy.35
  315.1 0.1 fusion.8
  315.1 0.9 broadcast_multiply_fusion.1
  316.1 0.0 all-gather.7.cloned.1.call-update
  316.1 0.0 all-gather.9.cloned.1.call-start
  316.2 0.3 copy.36
  316.4 0.9 broadcast_multiply_fusion
  317.4 0.0 all-gather.9.cloned.1.call-update
  317.4 0.0 all-gather.11.cloned.1.call-start
  317.5 66.2 %all-gather.7.cloned.1.call-done = f32[6144,256]{0,1:T(8,128)} async-done(((f32[768,256]{0,1:T(8,128)}), f32[6144,256]{0,1:T(8,128)}) %all-gather.7.cloned.1.call-update) | async-done | bytes 6291472 | tf_op jit(solution)/shard_map/all_gather | solution.py:35
  383.7 3.9 dynamic-slice_select_fusion.1
  387.6 0.0 all-gather.11.cloned.1.call-update
  387.6 0.0 all-gather.13.cloned.1.call-start
  387.7 61.5 %all-gather.9.cloned.1.call-done = f32[6144,256]{0,1:T(8,128)} async-done(((f32[768,256]{0,1:T(8,128)}), f32[6144,256]{0,1:T(8,128)}) %all-gather.9.cloned.1.call-update) | async-done | bytes 6291472 | tf_op jit(solution)/shard_map/all_gather | solution.py:35
  449.2 3.8 dynamic-slice_select_fusion
  453.1 0.0 all-gather.13.cloned.1.call-update
  453.1 0.0 reduce-scatter.3.cloned.1.call-start
  453.1 119.0 %all-gather.11.cloned.1.call-done = f32[12288,256]{0,1:T(8,128)} async-done(((f32[3072,256]{0,1:T(8,128)}), f32[12288,256]{0,1:T(8,128)}) %all-gather.11.cloned.1.call-update) | async-done | bytes 12582928 | tf_op jit(solution)/shard_map/all_gather | solution.py:12
  572.1 15.9 %reshape.115 = f32[4,3072,256]{1,0,2:T(4,128)} reshape(f32[12288,256]{0,1:T(8,128)} %all-gather.11.cloned.1.call-done) | data formatting | bytes 25165824 | tf_op jit(solution)/shard_map/all_gather | solution.py:12
  588.1 9.9 reduce_sum.18
  597.9 70.2 %convolution_bitcast_fusion.1 = f32[6144,256]{0,1:T(8,128)} fusion(f32[3072,256]{0,1:T(8,128)S(1)} %reduce_sum.18, f32[6144,3072]{1,0:T(8,128)} %param.14), kind=kOutput, calls=%fused_computation.4 | convolution fusion | flops 57982058496 | bytes 84934656 | tf_op jit(solution)/shard_map/dot_general | solution.py:16
  668.1 0.0 reduce-scatter.3.cloned.1.call-update
  668.1 0.0 reduce-scatter.5.cloned.1.call-start
  668.2 28.1 %all-gather.13.cloned.1.call-done = f32[12288,256]{0,1:T(8,128)} async-done(((f32[3072,256]{0,1:T(8,128)}), f32[12288,256]{0,1:T(8,128)}) %all-gather.13.cloned.1.call-update) | async-done | bytes 12582928 | tf_op jit(solution)/shard_map/all_gather | solution.py:12
  696.3 15.5 %reshape.116 = f32[4,3072,256]{1,0,2:T(4,128)} reshape(f32[12288,256]{0,1:T(8,128)} %all-gather.13.cloned.1.call-done) | data formatting | bytes 25165824 | tf_op jit(solution)/shard_map/all_gather | solution.py:12
  711.8 10.0 reduce_sum.19
  721.8 70.1 %convolution_bitcast_fusion = f32[6144,256]{0,1:T(8,128)} fusion(f32[3072,256]{0,1:T(8,128)S(1)} %reduce_sum.19, f32[6144,3072]{1,0:T(8,128)} %param.14), kind=kOutput, calls=%fused_computation.3 | convolution fusion | flops 57982058496 | bytes 84934656 | tf_op jit(solution)/shard_map/dot_general | solution.py:16
  791.8 0.0 reduce-scatter.5.cloned.1.call-update
  791.9 0.3 all-reduce.5.cloned.1.call-start
  792.2 0.0 reduce-scatter.3.cloned.1.call-done
  792.2 1.4 multiply_negate_fusion
  793.6 1.5 fusion.11
  795.1 1.5 fusion.10
  796.7 65.1 %reduce-scatter.5.cloned.1.call-done = f32[768,256]{0,1:T(8,128)} async-done(((f32[6144,256]{0,1:T(8,128)}), f32[768,256]{0,1:T(8,128)}) %reduce-scatter.5.cloned.1.call-update) | async-done | bytes 786448 | tf_op jit(solution)/shard_map/reduce_scatter | solution.py:38
  861.8 2.7 fusion.12
  864.4 0.0 all-reduce.5.cloned.1.call-update
  864.5 0.1 copy.38
  864.6 1.1 copy.41
  865.8 2.0 fusion.1
  867.8 1.1 copy.42
  868.9 128.6 %all-reduce.5.cloned.1.call-done = (f32[256,256]{1,0:T(8,128)}, f32[256,256]{1,0:T(8,128)}, f32[256,256]{0,1:T(8,128)}) async-done(((f32[256,256]{1,0:T(8,128)}, f32[256,256]{1,0:T(8,128)}, f32[256,256]{0,1:T(8,128)}), (f32[256,256]{1,0:T(8,128)}, f32[256,256]{1,0:T(8,128)}, f32[256,256]{0,1:T(8,128)})) %all-reduce.5.cloned.1.call-update) | async-done | bytes 786448 | tf_op jit(solution)/shard_map/psum | solution.py:69
  997.5 1.0 sub.20
  998.5 0.0 copy-start.5
  998.5 1.4 fusion.4
  999.9 0.0 copy-start.6
  999.9 0.6 fusion.3
  1000.6 1.6 fusion.2
  1002.2 0.8 copy.43
  (26 shorter events, 0.2 us)
Async XLA Ops:
  7.2 858.6 %copy-start = (f32[256,256]{1,0:T(8,128)S(1)}, f32[256,256]{1,0:T(8,128)}, u32[]{:S(2)}) copy-start(f32[256,256]{1,0:T(8,128)} %param.17) | copy-start | bytes 786436
  7.2 3.9 copy-start.1
  7.2 376.5 %all-gather.7.cloned.1.call-start = ((), (), s32[]{:S(2)}) async-start(), calls=%async_computation.2 | async-start | bytes 7077888 | tf_op jit(solution)/shard_map/all_gather | solution.py:35
  11.1 151.8 %copy-start.2 = (s32[192]{0:T(256)S(1)}, s32[192]{0:T(256)}, u32[]{:S(2)}) copy-start(s32[192]{0:T(256)} %param.21) | copy-start | bytes 2308
  162.9 151.8 %copy-start.7 = (f32[768,256]{1,0:T(8,128)S(1)}, f32[768,256]{1,0:T(8,128)}, u32[]{:S(2)}) copy-start(f32[768,256]{1,0:T(8,128)} %param.15) | copy-start | bytes 2359300
  162.9 153.2 %copy-start.8 = (f32[768,256]{1,0:T(8,128)S(1)}, f32[768,256]{1,0:T(8,128)}, u32[]{:S(2)}) copy-start(f32[768,256]{1,0:T(8,128)} %param.16) | copy-start | bytes 2359300
  316.1 133.1 %all-gather.9.cloned.1.call-start = ((), (), s32[]{:S(2)}) async-start(), calls=%async_computation.4 | async-start | bytes 7077888 | tf_op jit(solution)/shard_map/all_gather | solution.py:35
  317.4 254.7 %all-gather.11.cloned.1.call-start = ((), (), s32[]{:S(2)}) async-start(), calls=%async_computation.6 | async-start | bytes 15728640 | tf_op jit(solution)/shard_map/all_gather | solution.py:12
  387.6 308.6 %all-gather.13.cloned.1.call-start = ((), (), s32[]{:S(2)}) async-start(), calls=%async_computation.7 | async-start | bytes 15728640 | tf_op jit(solution)/shard_map/all_gather | solution.py:12
  453.1 339.1 %reduce-scatter.3.cloned.1.call-start = ((), (), s32[]{:S(2)}) async-start(), calls=%async_computation.3 | async-start | bytes 7077888 | tf_op jit(solution)/shard_map/reduce_scatter | solution.py:38
  668.1 193.7 %reduce-scatter.5.cloned.1.call-start = ((), (), s32[]{:S(2)}) async-start(), calls=%async_computation.5 | async-start | bytes 7077888 | tf_op jit(solution)/shard_map/reduce_scatter | solution.py:38
  791.8 1.7 copy-start.3
  791.8 3.3 copy-start.4
  791.8 72.6 %copy-start.10 = (f32[256,256]{1,0:T(8,128)S(1)}, f32[256,256]{1,0:T(8,128)}, u32[]{:S(2)}) copy-start(f32[256,256]{1,0:T(8,128)} %param.19) | copy-start | bytes 786436
  791.9 205.6 %all-reduce.5.cloned.1.call-start = ((), (), s32[]{:S(2)}) async-start(), calls=%async_computation.8 | async-start | bytes 1572864 | tf_op jit(solution)/shard_map/psum | solution.py:69
  793.6 203.9 %copy-start.9 = (f32[256,256]{1,0:T(8,128)S(1)}, f32[256,256]{1,0:T(8,128)}, u32[]{:S(2)}) copy-start(f32[256,256]{1,0:T(8,128)} %param.18) | copy-start | bytes 786436
  998.5 4.5 copy-start.5
  999.9 3.1 copy-start.6
Sparse Core Ops, SparseCore 0:
  316.2 67.4 all-gather.6
  385.9 63.3 all-gather.8
  451.1 121.0 all-gather.10
  573.8 122.3 all-gather.12
  698.4 69.7 reduce-scatter.2
  792.0 69.7 reduce-scatter.4
  867.9 129.5 all-reduce.4
